TPU v7x, 512 devices: a whole 4x4x16 slice. The times are simulated.
512 devices in a mesh: ctx: 32 (over x, y, core), head: 16 (over z).
Axes of the slice: x: 4, y: 4, z: 16, core: 2. Of those that a mesh axis runs over, the one named last changes fastest.
Arguments:
- mixed_in: bfloat16 [8192, 8192], P(('ctx', 'head')), may hold values from -6 to 6
- conv_weight: float32 [4, 8192], P(None, 'head'), may hold values from -3 to 3
- write_strength_logit: float32 [32, 8192], P('head', 'ctx'), may hold values from -10.5 to 2.2, as said below
- decay_log: float32 [32, 8192], P('head', 'ctx'), may hold values from -0.7 to 0, as said below
- initial_state: float32 [32, 128, 128], P('head'), may hold values from -6 to 6
- final_state_grad: float32 [32, 128, 128], P('head'), may hold values from -6 to 6
- grad_out: bfloat16 [8192, 4096], P('ctx', 'head'), may hold values from -6 to 6
Outputs:
- grad_mixed: bfloat16 [8192, 8192], P(('ctx', 'head'))
- grad_conv: float32 [4, 8192], P(None, 'head')
- grad_beta_logit: float32 [32, 8192], P('head', 'ctx')
- grad_decay_log: float32 [32, 8192], P('head', 'ctx')
Inputs may be any that keep to these rules, and one draw needn't show every extreme that they name: `write_strength_logit`: each value head's write strengths and decays vary from token to token. `decay_log`: every entry is negative.
All inputs are finite; a program needn't handle non-finite values.
Results may differ from a plain program's by a relative error of at most 0.001.
Values may be sent and summed in bfloat16 or wider, within the bound.
A program may use at most 64 MiB of HBM per device.

v0:
```python
import jax
import jax.numpy as jnp
from jax import lax
from jax.sharding import PartitionSpec as P

HK = 16
VALUE_HEADS = 32
DK = 128
DV = 128
KW = 4
BLOCK = 64
highest = lax.Precision.HIGHEST
norm_eps = 1e-06


def from_behind(value, axis, by):
    devices = lax.axis_size(axis)
    pairs = [(i, i + by) for i in range(devices) if 0 <= i + by < devices]
    return lax.ppermute(value, axis, pairs)


def prefix(value, axis, combine, identity, reverse):
    devices, mine = (lax.axis_size(axis), lax.axis_index(axis))
    everything = jax.tree.map(lambda part: lax.all_gather(part, axis), value)
    start = jax.tree.map(
        lambda part, zero: jnp.broadcast_to(jnp.asarray(zero, part.dtype), part.shape),
        value,
        identity,
    )

    def step(k, before):
        at = devices - 1 - k if reverse else k
        reached = at > mine if reverse else at < mine
        new = combine(before, jax.tree.map(lambda part: part[at], everything))
        return jax.tree.map(lambda a, b: jnp.where(reached, a, b), new, before)

    return lax.fori_loop(0, devices, step, start)


def block_step(carried, pieces):
    state, transit = carried
    queries, key_feats, values, beta_gate, log_decay = pieces
    block_size = log_decay.shape[0]
    cumulative = jnp.cumsum(log_decay)
    row_ids = lax.broadcasted_iota(jnp.int32, (block_size, block_size), 0)
    col_ids = lax.broadcasted_iota(jnp.int32, (block_size, block_size), 1)
    causal = col_ids <= row_ids
    differ = jnp.where(causal, cumulative[:, None] - cumulative[None, :], 0.0)
    ratios = jnp.where(causal, jnp.exp(differ), 0.0)
    key_gram = jnp.dot(key_feats, key_feats.T, precision=highest)
    lower_part = jnp.where(col_ids < row_ids, beta_gate[:, None] * ratios * key_gram, 0.0)
    system = lower_part + jnp.eye(block_size, dtype=jnp.float32)
    decays = jnp.exp(cumulative)
    right_sides = jnp.concatenate(
        [beta_gate[:, None] * values, (beta_gate * decays)[:, None] * key_feats], axis=1
    )
    solved = jax.scipy.linalg.solve_triangular(system, right_sides, lower=True)
    width_v = values.shape[1]
    base_update = solved[:, :width_v]
    weights = solved[:, width_v:]
    update = base_update - jnp.dot(weights, state, precision=highest)
    scores = ratios * jnp.dot(queries, key_feats.T, precision=highest)
    output = decays[:, None] * jnp.dot(queries, state, precision=highest) + jnp.dot(
        scores, update, precision=highest
    )
    total_decay = jnp.exp(cumulative[-1])
    tail_keys = jnp.exp(cumulative[-1] - cumulative)[:, None] * key_feats
    new_state = total_decay * state + jnp.dot(tail_keys.T, update, precision=highest)
    step_map = total_decay * jnp.eye(key_feats.shape[1], dtype=jnp.float32) - jnp.dot(
        tail_keys.T, weights, precision=highest
    )
    new_transit = jnp.dot(step_map, transit, precision=highest)
    return ((new_state, new_transit), output)


def run_head(state, queries, key_feats, values, beta_gate, log_decay):
    blocks = queries.shape[0] // BLOCK
    pieces = (
        queries.reshape(blocks, BLOCK, -1),
        key_feats.reshape(blocks, BLOCK, -1),
        values.reshape(blocks, BLOCK, -1),
        beta_gate.reshape(blocks, BLOCK),
        log_decay.reshape(blocks, BLOCK),
    )
    start = (state, jnp.eye(key_feats.shape[1], dtype=jnp.float32))
    (state_end, transit), outputs = lax.scan(block_step, start, pieces)
    return (outputs.reshape(-1, values.shape[1]), state_end, transit)


def normalize(feats, factor):
    return feats * lax.rsqrt(jnp.sum(feats * feats, axis=-1, keepdims=True) + norm_eps) * factor


def mix_layer(state_in, extended, conv_weight, write_strength_logit, decay_log):
    row_count = extended.shape[0] - (KW - 1)
    filtered_signal = conv_weight[0] * extended[0:row_count]
    for tap in range(1, KW):
        filtered_signal = filtered_signal + conv_weight[tap] * extended[tap : tap + row_count]
    activated = jax.nn.silu(filtered_signal)
    ratio_heads = VALUE_HEADS // HK
    group_width = 2 * DK + ratio_heads * DV
    groups = activated.reshape(row_count, -1, group_width)
    key_heads = groups.shape[1]
    queries = normalize(groups[:, :, :DK], DK ** (-0.5))
    key_feats = normalize(groups[:, :, DK : 2 * DK], 1.0)
    values = (
        groups[:, :, 2 * DK :].reshape(row_count, key_heads * ratio_heads, DV).transpose(1, 0, 2)
    )
    queries = jnp.repeat(queries.transpose(1, 0, 2), ratio_heads, axis=0)
    key_feats = jnp.repeat(key_feats.transpose(1, 0, 2), ratio_heads, axis=0)
    beta_gate = jax.nn.sigmoid(write_strength_logit)
    outputs, state_out, transit = jax.vmap(run_head)(
        state_in, queries, key_feats, values, beta_gate, decay_log
    )
    result = outputs.transpose(1, 0, 2).reshape(row_count, -1)
    return ((result, state_out), transit)


def compose(earlier, later):
    matrix = jnp.einsum("hij,hjk->hik", later[0], earlier[0], precision=highest)
    offset = jnp.einsum("hij,hjk->hik", later[0], earlier[1], precision=highest) + later[1]
    return (matrix, offset)


def advance(maps, state):
    return jnp.einsum("hij,hjk->hik", maps[0], state, precision=highest) + maps[1]


def on_device(
    mixed_in,
    conv_weight,
    write_strength_logit,
    decay_log,
    initial_state,
    final_state_grad,
    grad_out,
):
    local_in = lax.all_to_all(mixed_in, "head", split_axis=1, concat_axis=0, tiled=True)
    edge_rows = from_behind(local_in[-(KW - 1) :], "ctx", 1)
    extended = jnp.concatenate([edge_rows, local_in], axis=0).astype(jnp.float32)
    cotangent = grad_out.astype(jnp.float32)
    zeros_state = jnp.zeros_like(initial_state)

    def from_state(state):
        return mix_layer(state, extended, conv_weight, write_strength_logit, decay_log)

    primal, pull_state, transit = jax.vjp(from_state, zeros_state, has_aux=True)
    offset = primal[1]
    local_grad = pull_state((cotangent, jnp.zeros_like(offset)))[0]
    flipped = jnp.swapaxes(transit, 1, 2)
    identity = (
        jnp.broadcast_to(jnp.eye(transit.shape[1], dtype=jnp.float32), transit.shape),
        jnp.zeros_like(offset),
    )
    earlier_map = prefix((transit, offset), "ctx", compose, identity, False)
    later_map = prefix((flipped, local_grad), "ctx", compose, identity, True)
    state_in = advance(earlier_map, initial_state)
    state_grad = advance(later_map, final_state_grad)

    def forward(ext_rows, weight_taps, logits, decay_logs):
        return mix_layer(state_in, ext_rows, weight_taps, logits, decay_logs)

    unused, pull_all, unused_transit = jax.vjp(
        forward, extended, conv_weight, write_strength_logit, decay_log, has_aux=True
    )
    grad_ext, grad_weight, grad_beta, grad_decay = pull_all((cotangent, state_grad))
    spilled = from_behind(grad_ext[: KW - 1], "ctx", -1)
    own_grad = grad_ext[KW - 1 :]
    own_grad = jnp.concatenate([own_grad[: -(KW - 1)], own_grad[-(KW - 1) :] + spilled], axis=0)
    returned = lax.all_to_all(
        own_grad.astype(jnp.bfloat16), "head", split_axis=0, concat_axis=1, tiled=True
    )
    weight_total = lax.psum(grad_weight, "ctx")
    return (returned, weight_total, grad_beta, grad_decay)


def solution(mesh):
    in_specs = (
        P(("ctx", "head"), None),
        P(None, "head"),
        P("head", "ctx"),
        P("head", "ctx"),
        P("head", None, None),
        P("head", None, None),
        P("ctx", "head"),
    )
    out_specs = (P(("ctx", "head"), None), P(None, "head"), P("head", "ctx"), P("head", "ctx"))
    return jax.shard_map(
        on_device, mesh=mesh, in_specs=in_specs, out_specs=out_specs, check_vma=False
    )
```

profile of v0, /device:TPU:32, one launch (start us, length us, event | category | flops | bytes accessed | tf_op | source)
XLA Modules:
  0.0 795.1 jit_solution(5155768118002871086)
XLA Ops:
  8.9 15.2 %all-to-all-start = ((bf16[16,16,512]{2,0,1:T(8,128)(2,1)}), bf16[16,16,512]{2,0,1:T(8,128)(2,1)S(1)}, u32[]{:S(2)}, u32[]{:S(2)}) async-start(bf16[16,16,512]{2,0,1:T(8,128)(2,1)} %bitcast.435), calls=%async_computation | async-start | bytes 524288 | tf_op jit(solution)/shard_map/all_to_all | solution.py:138
  26.4 15.6 %all-to-all-done = bf16[16,16,512]{2,0,1:T(8,128)(2,1)S(1)} async-done(((bf16[16,16,512]{2,0,1:T(8,128)(2,1)}), bf16[16,16,512]{2,0,1:T(8,128)(2,1)S(1)}, u32[]{:S(2)}, u32[]{:S(2)}) %all-to-all-start) | async-done | bytes 262176 | tf_op jit(solution)/shard_map/all_to_all | solution.py:138
  48.5 65.6 %while.169 = (s32[]{:T(128)}, f32[2,128,128]{2,1,0:T(8,128)S(1)}, f32[2,128,128]{2,1,0:T(8,128)S(1)}, f32[4,2,64,128]{3,2,1,0:T(8,128)S(1)}, f32[4,2,64,1]{2,1,3...) while((s32[]{:T(128)}, f32[2,128,128]{2,1,0:T(8,128)S(1)}, ...), condition=%wide.region_4.6_spmd.clone.clone, body=%wide.region_2.5_spmd.clone.clone.sunk | while | flops 176640128 | bytes 2980628 | solution.py:86
  51.5 9.8 %custom-call.35 = f32[2,1,64,64]{2,3,1,0:T(8,128)S(1)} custom-call(f32[2,1,64,64]{3,2,1,0:T(8,128)S(1)} %fusion.420), custom_call_target="InvertDiagBlocksLowerTriangular" | custom-call | tf_op jit(solution)/shard_map/jvp(vmap())/while/body/eval_jaxpr/jit(_solve_triangular)/triangular_solve/custom-call.1 | solution.py:57
  67.9 9.8 %custom-call.35 = f32[2,1,64,64]{2,3,1,0:T(8,128)S(1)} custom-call(f32[2,1,64,64]{3,2,1,0:T(8,128)S(1)} %fusion.420), custom_call_target="InvertDiagBlocksLowerTriangular" | custom-call | tf_op jit(solution)/shard_map/jvp(vmap())/while/body/eval_jaxpr/jit(_solve_triangular)/triangular_solve/custom-call.1 | solution.py:57
  84.2 9.8 %custom-call.35 = f32[2,1,64,64]{2,3,1,0:T(8,128)S(1)} custom-call(f32[2,1,64,64]{3,2,1,0:T(8,128)S(1)} %fusion.420), custom_call_target="InvertDiagBlocksLowerTriangular" | custom-call | tf_op jit(solution)/shard_map/jvp(vmap())/while/body/eval_jaxpr/jit(_solve_triangular)/triangular_solve/custom-call.1 | solution.py:57
  100.7 9.8 %custom-call.35 = f32[2,1,64,64]{2,3,1,0:T(8,128)S(1)} custom-call(f32[2,1,64,64]{3,2,1,0:T(8,128)S(1)} %fusion.420), custom_call_target="InvertDiagBlocksLowerTriangular" | custom-call | tf_op jit(solution)/shard_map/jvp(vmap())/while/body/eval_jaxpr/jit(_solve_triangular)/triangular_solve/custom-call.1 | solution.py:57
  116.9 9.2 %while.166 = (s32[]{:T(128)}, f32[2,128,128]{2,1,0:T(8,128)S(1)}, f32[4,2,1,1]{1,3,2,0:T(1,128)S(1)}, f32[4,2,64,128]{3,2,1,0:T(8,128)S(1)}, f32[4,2,64,1]{2,1,3...) while((s32[]{:T(128)}, f32[2,128,128]{2,1,0:T(8,128)S(1)}, ...), condition=%wide.region_6.8_spmd.clone, body=%wide.region_5.7_spmd.clone.sunk | while | flops 88293376 | bytes 1316019 | solution.py:86
  128.2 45.1 %all-gather.9.cloned.1.call-done = f32[64,128,128]{2,1,0:T(8,128)} async-done(((f32[2,128,128]{2,1,0:T(8,128)}), f32[64,128,128]{2,1,0:T(8,128)}) %all-gather.9.cloned.1.call-update) | async-done | bytes 4194320 | tf_op jit(solution)/shard_map/all_gather | solution.py:24
  173.2 64.6 %all-gather.11.cloned.1.call-done = f32[64,128,128]{2,1,0:T(8,128)} async-done(((f32[2,128,128]{2,1,0:T(8,128)}), f32[64,128,128]{2,1,0:T(8,128)}) %all-gather.11.cloned.1.call-update) | async-done | bytes 4194320 | tf_op jit(solution)/shard_map/all_gather | solution.py:24
  237.9 80.1 %while.167 = (s32[]{:T(128)}, f32[2,128,128]{2,1,0:T(8,128)S(1)}, f32[2,128,128]{2,1,0:T(8,128)S(1)}, s32[]{:T(128)}, f32[32,2,128,128]{3,2,1,0:T(8,128)}, /*ind...) while((s32[]{:T(128)}, f32[2,128,128]{2,1,0:T(8,128)S(1)}, ...), condition=%wide.region_8.10_spmd.clone, body=%wide.region_7.9_spmd.clone.sunk | while | flops 100827144 | bytes 1706674 | solution.py:37
  318.0 47.8 %all-gather.15.cloned.1.call-done = f32[64,128,128]{2,1,0:T(8,128)} async-done(((f32[2,128,128]{2,1,0:T(8,128)}), f32[64,128,128]{2,1,0:T(8,128)}) %all-gather.15.cloned.1.call-update) | async-done | bytes 4194320 | tf_op jit(solution)/shard_map/all_gather | solution.py:24
  365.9 79.6 %while.168 = (s32[]{:T(128)}, f32[2,128,128]{2,1,0:T(8,128)S(1)}, f32[2,128,128]{2,1,0:T(8,128)S(1)}, s32[]{:T(128)}, f32[32,2,128,128]{3,2,1,0:T(8,128)}, /*ind...) while((s32[]{:T(128)}, f32[2,128,128]{2,1,0:T(8,128)S(1)}, f32[2,128,128]{2,1,0:T(8,128)S(1)}, ...), condition=%wide.region_10.12_spmd.clone, body=%wide.region_9.11_spmd.clone.sunk | while | flops 100827136 | bytes 1706612 | solution.py:37
  458.0 107.3 %while.164 = (s32[]{:T(128)}, f32[2,128,128]{2,1,0:T(8,128)S(1)}, f32[4,2,64,64]{3,2,1,0:T(8,128)}, f32[4,2,128,64]{2,3,1,0:T(8,128)}, f32[4,2,64,64]{3,2,1,0:T(...) while((s32[]{:T(128)}, f32[2,128,128]{2,1,0:T(8,128)S(1)}, ...), condition=%wide.region_13.15_spmd.clone.clone, body=%wide.region_11.14_spmd.clone.clone.sunk | while | flops 126194176 | bytes 3312057 | solution.py:86
  463.0 11.2 %custom-call.33 = f32[2,1,64,64]{2,3,1,0:T(8,128)} custom-call(f32[2,1,64,64]{3,2,1,0:T(8,128)} %select_bitcast_fusion.4), custom_call_target="InvertDiagBlocksLowerTriangular" | custom-call | tf_op jit(solution)/shard_map/jvp(vmap())/while/body/eval_jaxpr/jit(_solve_triangular)/triangular_solve/custom-call.1 | solution.py:57
  474.2 1.8 bitcast_dynamic-update-slice_fusion.22
  489.8 11.2 %custom-call.33 = f32[2,1,64,64]{2,3,1,0:T(8,128)} custom-call(f32[2,1,64,64]{3,2,1,0:T(8,128)} %select_bitcast_fusion.4), custom_call_target="InvertDiagBlocksLowerTriangular" | custom-call | tf_op jit(solution)/shard_map/jvp(vmap())/while/body/eval_jaxpr/jit(_solve_triangular)/triangular_solve/custom-call.1 | solution.py:57
  501.0 1.8 bitcast_dynamic-update-slice_fusion.22
  516.6 11.2 %custom-call.33 = f32[2,1,64,64]{2,3,1,0:T(8,128)} custom-call(f32[2,1,64,64]{3,2,1,0:T(8,128)} %select_bitcast_fusion.4), custom_call_target="InvertDiagBlocksLowerTriangular" | custom-call | tf_op jit(solution)/shard_map/jvp(vmap())/while/body/eval_jaxpr/jit(_solve_triangular)/triangular_solve/custom-call.1 | solution.py:57
  527.8 1.8 bitcast_dynamic-update-slice_fusion.22
  543.5 11.2 %custom-call.33 = f32[2,1,64,64]{2,3,1,0:T(8,128)} custom-call(f32[2,1,64,64]{3,2,1,0:T(8,128)} %select_bitcast_fusion.4), custom_call_target="InvertDiagBlocksLowerTriangular" | custom-call | tf_op jit(solution)/shard_map/jvp(vmap())/while/body/eval_jaxpr/jit(_solve_triangular)/triangular_solve/custom-call.1 | solution.py:57
  554.7 1.8 bitcast_dynamic-update-slice_fusion.22
  569.3 127.3 %while.165 = (s32[]{:T(128)}, f32[2,128,128]{2,1,0:T(8,128)S(1)}, f32[4,2,64,128]{3,2,1,0:T(8,128)}, f32[4,2,64,128]{3,2,1,0:T(8,128)}, f32[4,2,64,128]{3,2,0,1:...) while((s32[]{:T(128)}, f32[2,128,128]{2,1,0:T(8,128)S(1)}, ...), condition=%wide.region_25.27_spmd.clone.clone, body=%wide.region_14.26_spmd.clone.clone.sunk | while | flops 283857920 | bytes 5617773 | solution.py:86
  572.9 9.8 %custom-call.34 = f32[2,1,64,64]{2,3,1,0:T(8,128)S(1)} custom-call(f32[2,1,64,64]{3,2,1,0:T(8,128)S(1)} %select_bitcast_fusion.5), custom_call_target="InvertDiagBlocksLowerTriangular" | custom-call | tf_op jit(solution)/shard_map/transpose(jvp(vmap()))/while/body/eval_jaxpr/jit(_solve_triangular)/triangular_solve | solution.py:57
  594.8 1.8 fusion.380
  604.8 9.8 %custom-call.34 = f32[2,1,64,64]{2,3,1,0:T(8,128)S(1)} custom-call(f32[2,1,64,64]{3,2,1,0:T(8,128)S(1)} %select_bitcast_fusion.5), custom_call_target="InvertDiagBlocksLowerTriangular" | custom-call | tf_op jit(solution)/shard_map/transpose(jvp(vmap()))/while/body/eval_jaxpr/jit(_solve_triangular)/triangular_solve | solution.py:57
  626.6 1.8 fusion.380
  636.6 9.8 %custom-call.34 = f32[2,1,64,64]{2,3,1,0:T(8,128)S(1)} custom-call(f32[2,1,64,64]{3,2,1,0:T(8,128)S(1)} %select_bitcast_fusion.5), custom_call_target="InvertDiagBlocksLowerTriangular" | custom-call | tf_op jit(solution)/shard_map/transpose(jvp(vmap()))/while/body/eval_jaxpr/jit(_solve_triangular)/triangular_solve | solution.py:57
  658.5 1.8 fusion.380
  668.4 9.8 %custom-call.34 = f32[2,1,64,64]{2,3,1,0:T(8,128)S(1)} custom-call(f32[2,1,64,64]{3,2,1,0:T(8,128)S(1)} %select_bitcast_fusion.5), custom_call_target="InvertDiagBlocksLowerTriangular" | custom-call | tf_op jit(solution)/shard_map/transpose(jvp(vmap()))/while/body/eval_jaxpr/jit(_solve_triangular)/triangular_solve | solution.py:57
  707.4 12.7 %all-to-all-start.1 = ((bf16[16,16,512]{2,1,0:T(8,128)(2,1)}), bf16[16,16,512]{2,1,0:T(8,128)(2,1)S(1)}, u32[]{:S(2)}, u32[]{:S(2)}) async-start(bf16[16,16,512]{2,1,0:T(8,128)(2,1)} %bitcast.32), calls=%async_computation.1 | async-start | bytes 524288 | tf_op jit(solution)/shard_map/all_to_all | solution.py:170
  720.8 66.5 %psum.7 = f32[4,512]{1,0:T(4,128)} all-reduce(f32[4,512]{1,0:T(4,128)S(1)} %pad_add_fusion.5), channel_id=1, replica_groups=mesh['ctx'=32,'head'=16] {'ctx'}, use_global_device_ids=true, to_apply=%region_34.36 | all-reduce | flops 2048 | bytes 16384 | tf_op jit(solution)/shard_map/psum | solution.py:173
  (740 shorter events, 372.2 us)
Async XLA Ops:
  7.2 438.4 %copy-start = (f32[2,128,128]{2,1,0:T(8,128)S(1)}, f32[2,128,128]{2,1,0:T(8,128)}, u32[]{:S(2)}) copy-start(f32[2,128,128]{2,1,0:T(8,128)} %param.25) | copy-start | bytes 393220
  8.9 33.1 %all-to-all-start = ((bf16[16,16,512]{2,0,1:T(8,128)(2,1)}), bf16[16,16,512]{2,0,1:T(8,128)(2,1)S(1)}, u32[]{:S(2)}, u32[]{:S(2)}) async-start(bf16[16,16,512]{2,0,1:T(8,128)(2,1)} %bitcast.435), calls=%async_computation | async-start | bytes 524288 | tf_op jit(solution)/shard_map/all_to_all | solution.py:138
  24.1 149.1 %all-gather.9.cloned.1.call-start = ((), (), s32[]{:S(2)}) async-start(), calls=%async_computation.2 | async-start | bytes 4325376 | tf_op jit(solution)/shard_map/all_gather | solution.py:24
  26.3 21.4 %copy-start.8 = (f32[1,512]{1,0:T(1,128)}, f32[1,512]{1,0:T(1,128)S(1)}, u32[]{:S(2)}) copy-start(f32[1,512]{1,0:T(1,128)S(1)} %get-tuple-element.3118) | copy-start | bytes 6148
  26.3 21.4 %copy-start.10 = (f32[1,512]{1,0:T(1,128)}, f32[1,512]{1,0:T(1,128)S(1)}, u32[]{:S(2)}) copy-start(f32[1,512]{1,0:T(1,128)S(1)} %get-tuple-element.3119) | copy-start | bytes 6148
  26.3 21.4 %copy-start.12 = (f32[1,512]{1,0:T(1,128)}, f32[1,512]{1,0:T(1,128)S(1)}, u32[]{:S(2)}) copy-start(f32[1,512]{1,0:T(1,128)S(1)} %get-tuple-element.3120) | copy-start | bytes 6148
  26.4 21.4 %copy-start.14 = (f32[1,512]{1,0:T(1,128)}, f32[1,512]{1,0:T(1,128)S(1)}, u32[]{:S(2)}) copy-start(f32[1,512]{1,0:T(1,128)S(1)} %get-tuple-element.3121) | copy-start | bytes 6148
  42.0 3.4 collective-permute-start
  46.7 1.8 copy-start.19
  48.5 66.4 %copy-start.5 = (bf16[256,256]{1,0:T(8,128)(2,1)S(1)}, bf16[256,256]{1,0:T(8,128)(2,1)}, u32[]{:S(2)}) copy-start(bf16[256,256]{1,0:T(8,128)(2,1)} %param.27) | copy-start | bytes 393220
  114.1 2.8 copy-start.2
  114.1 2.8 copy-start.3
  114.9 123.0 %all-gather.11.cloned.1.call-start = ((), (), s32[]{:S(2)}) async-start(), calls=%async_computation.3 | async-start | bytes 4325376 | tf_op jit(solution)/shard_map/all_gather | solution.py:24
  126.8 191.2 %all-gather.13.cloned.1.call-start = ((), (), s32[]{:S(2)}) async-start(), calls=%async_computation.4 | async-start | bytes 4325376 | tf_op jit(solution)/shard_map/all_gather | solution.py:24
  127.6 238.3 %all-gather.15.cloned.1.call-start = ((), (), s32[]{:S(2)}) async-start(), calls=%async_computation.5 | async-start | bytes 4325376 | tf_op jit(solution)/shard_map/all_gather | solution.py:24
  318.0 47.9 %copy-start.4 = (f32[2,128,128]{2,1,0:T(8,128)}, f32[2,128,128]{2,1,0:T(8,128)S(1)}, u32[]{:S(2)}) copy-start(f32[2,128,128]{2,1,0:T(8,128)S(1)} %get-tuple-element.2004) | copy-start | bytes 393220
  569.3 29.8 %copy-start.7 = (f32[4,2,64]{2,1,0:T(2,128)S(1)}, f32[4,2,64]{2,1,0:T(2,128)}, u32[]{:S(2)}) copy-start(f32[4,2,64]{2,1,0:T(2,128)} %get-tuple-element.4201) | copy-start | bytes 6148 | tf_op jit(solution)/shard_map/transpose(jvp(vmap()))/while
  569.3 30.1 %copy-start.6 = (f32[4,2,64]{2,1,0:T(2,128)S(1)}, f32[4,2,64]{2,1,0:T(2,128)}, u32[]{:S(2)}) copy-start(f32[4,2,64]{2,1,0:T(2,128)} %get-tuple-element.4198) | copy-start | bytes 6148 | tf_op jit(solution)/shard_map/transpose(jvp(vmap()))/while
  601.2 29.8 %copy-start.7 = (f32[4,2,64]{2,1,0:T(2,128)S(1)}, f32[4,2,64]{2,1,0:T(2,128)}, u32[]{:S(2)}) copy-start(f32[4,2,64]{2,1,0:T(2,128)} %get-tuple-element.4201) | copy-start | bytes 6148 | tf_op jit(solution)/shard_map/transpose(jvp(vmap()))/while
  601.2 30.0 %copy-start.6 = (f32[4,2,64]{2,1,0:T(2,128)S(1)}, f32[4,2,64]{2,1,0:T(2,128)}, u32[]{:S(2)}) copy-start(f32[4,2,64]{2,1,0:T(2,128)} %get-tuple-element.4198) | copy-start | bytes 6148 | tf_op jit(solution)/shard_map/transpose(jvp(vmap()))/while
  633.0 29.8 %copy-start.7 = (f32[4,2,64]{2,1,0:T(2,128)S(1)}, f32[4,2,64]{2,1,0:T(2,128)}, u32[]{:S(2)}) copy-start(f32[4,2,64]{2,1,0:T(2,128)} %get-tuple-element.4201) | copy-start | bytes 6148 | tf_op jit(solution)/shard_map/transpose(jvp(vmap()))/while
  633.0 30.0 %copy-start.6 = (f32[4,2,64]{2,1,0:T(2,128)S(1)}, f32[4,2,64]{2,1,0:T(2,128)}, u32[]{:S(2)}) copy-start(f32[4,2,64]{2,1,0:T(2,128)} %get-tuple-element.4198) | copy-start | bytes 6148 | tf_op jit(solution)/shard_map/transpose(jvp(vmap()))/while
  664.8 29.8 %copy-start.7 = (f32[4,2,64]{2,1,0:T(2,128)S(1)}, f32[4,2,64]{2,1,0:T(2,128)}, u32[]{:S(2)}) copy-start(f32[4,2,64]{2,1,0:T(2,128)} %get-tuple-element.4201) | copy-start | bytes 6148 | tf_op jit(solution)/shard_map/transpose(jvp(vmap()))/while
  664.8 30.1 %copy-start.6 = (f32[4,2,64]{2,1,0:T(2,128)S(1)}, f32[4,2,64]{2,1,0:T(2,128)}, u32[]{:S(2)}) copy-start(f32[4,2,64]{2,1,0:T(2,128)} %get-tuple-element.4198) | copy-start | bytes 6148 | tf_op jit(solution)/shard_map/transpose(jvp(vmap()))/while
  696.7 6.5 copy-start.9
  696.7 6.6 copy-start.11
  696.7 6.6 copy-start.13
  696.7 6.6 copy-start.15
  703.5 16.6 %copy-start.16 = (f32[4,2,64]{2,1,0:T(2,128)S(1)}, f32[4,2,64]{2,1,0:T(2,128)}, u32[]{:S(2)}) copy-start(f32[4,2,64]{2,1,0:T(2,128)} %get-tuple-element.2034) | copy-start | bytes 6148
  703.5 83.7 %copy-start.20 = (f32[2,256]{1,0:T(2,128)S(1)}, f32[2,256]{1,0:T(2,128)}, u32[]{:S(2)}) copy-start(f32[2,256]{1,0:T(2,128)} %param.23) | copy-start | bytes 6148
  703.6 3.1 collective-permute-start.1
  707.4 80.5 %all-to-all-start.1 = ((bf16[16,16,512]{2,1,0:T(8,128)(2,1)}), bf16[16,16,512]{2,1,0:T(8,128)(2,1)S(1)}, u32[]{:S(2)}, u32[]{:S(2)}) async-start(bf16[16,16,512]{2,1,0:T(8,128)(2,1)} %bitcast.32), calls=%async_computation.1 | async-start | bytes 524288 | tf_op jit(solution)/shard_map/all_to_all | solution.py:170
  (3 other events, 2.5 us)
Sparse Core Ops, SparseCore 0:
  115.0 58.1 all-gather.8
  176.9 60.8 all-gather.10
  241.0 60.9 all-gather.12
  304.9 60.8 all-gather.14
where the time goes:
time: 802 us; the launch traced here: 795 us
  matrix products  258 us (32%)
  other arithmetic  180 us (22%)
  waiting for transfers between devices  176 us (22%)
  blocking collectives  66.5 us (8%)
  local copies, waits for them, and re-layouts  64.8 us (8%)
  starting transfers between devices  30.8 us (4%)
  between operations  14.3 us (2%)
    all_gather x4, waiting for transfers between devices, prefix(): everything = jax.tree.map(lambda part: lax.all_gather(part, axis), value)  158 us
    another operation x32, other arithmetic, block_step(): solved = jax.scipy.linalg.solve_triangular(system, right_sides, lower=True)  133 us
    dot_general x64, matrix products, compose(): jnp.einsum('hij,hjk->hik', later[0], earlier[1], precision=highest)  79.3 us
    dot_general x64, matrix products, compose(): matrix = jnp.einsum('hij,hjk->hik', later[0], earlier[0], precision=highest)  75.2 us
    psum x1, blocking collectives, on_device(): weight_total = lax.psum(grad_weight, 'ctx')  66.5 us
    dynamic_update_slice x24, other arithmetic, run_head(): (state_end, transit), outputs = lax.scan(block_step, start, pieces)  18.8 us
    dot_general x16, matrix products, block_step(): scores = ratios * jnp.dot(queries, key_feats.T, precision=highest)  18.5 us
    dot_general x20, matrix products, block_step(): jnp.dot(tail_keys.T, update, precision=highest)  17.8 us
  transfers between devices with their start and end apart: 8, of which 5 were waited for; matrix products, arithmetic and copies ran while one was open for 12% of the time, Pallas kernels for 0%

commit v1 on v0

--- a/solution.py
+++ b/solution.py
@@ -135,7 +135,18 @@
     final_state_grad,
     grad_out,
 ):
-    local_in = lax.all_to_all(mixed_in, "head", split_axis=1, concat_axis=0, tiled=True)
+    a_next, far_arr = (lax.axis_size("head"), lax.axis_index("head"))
+    a_now = list(mixed_in.shape)
+    local_now = mixed_in.shape[1] // a_next
+    a_now[1] = local_now
+    reply = a_now[0]
+    a_now[0] = reply * a_next
+    local_in = jnp.zeros(a_now, mixed_in.dtype)
+    for nth in [*range(a_next)]:
+        val = lax.dynamic_slice_in_dim(mixed_in, (far_arr ^ nth) * local_now, local_now, axis=1)
+        if nth:
+            val = lax.ppermute(val, "head", perm=[(tick, tick ^ nth) for tick in range(a_next)])
+        local_in = lax.dynamic_update_slice_in_dim(local_in, val, (far_arr ^ nth) * reply, axis=0)
     edge_rows = from_behind(local_in[-(KW - 1) :], "ctx", 1)
     extended = jnp.concatenate([edge_rows, local_in], axis=0).astype(jnp.float32)
     cotangent = grad_out.astype(jnp.float32)

time: 802 us -> 858 us (1.070)
  starting transfers between devices: 30.8 us -> 96.9 us
    ppermute x0 -> x15, starting transfers between devices: none -> 81.3 us  [on_device(): lax.ppermute(val, 'head', perm=[(tick, tick ^ nth) for tick in range(a_ne...]
    all_to_all x1 -> x0, waiting for transfers between devices: 15.6 us -> none  [on_device(): lax.all_to_all(mixed_in, 'head', split_axis=1, concat_axis=0, tiled=True)]
    all_to_all x1 -> x0, starting transfers between devices: 15.2 us -> none  [on_device(): lax.all_to_all(mixed_in, 'head', split_axis=1, concat_axis=0, tiled=True)]
  transfers between devices with their start and end apart: 8 -> 22, of which waited for: 5 -> 5; matrix products, arithmetic and copies ran while one was open for 12% -> 11% of each run, Pallas kernels for 0% -> 0%
where the time goes in v1:
time: 858 us; the launch traced here: 851 us
  matrix products  255 us (30%)
  other arithmetic  178 us (21%)
  waiting for transfers between devices  170 us (20%)
  starting transfers between devices  96.9 us (11%)
  blocking collectives  66.4 us (8%)
  local copies, waits for them, and re-layouts  65 us (8%)
  between operations  14.8 us (2%)
    all_gather x4, waiting for transfers between devices, prefix(): everything = jax.tree.map(lambda part: lax.all_gather(part, axis), value)  162 us
    another operation x32, other arithmetic, block_step(): solved = jax.scipy.linalg.solve_triangular(system, right_sides, lower=True)  133 us
    ppermute x15, starting transfers between devices, on_device(): lax.ppermute(val, 'head', perm=[(tick, tick ^ nth) for tick in range(a_ne...  81.3 us
    dot_general x64, matrix products, compose(): jnp.einsum('hij,hjk->hik', later[0], earlier[1], precision=highest)  79.3 us
    dot_general x64, matrix products, compose(): matrix = jnp.einsum('hij,hjk->hik', later[0], earlier[0], precision=highest)  75.3 us
    psum x1, blocking collectives, on_device(): weight_total = lax.psum(grad_weight, 'ctx')  66.4 us
    dot_general x16, matrix products, block_step(): scores = ratios * jnp.dot(queries, key_feats.T, precision=highest)  18.5 us
  transfers between devices with their start and end apart: 22, of which 5 were waited for; matrix products, arithmetic and copies ran while one was open for 11% of the time, Pallas kernels for 0%

profile of v1, /device:TPU:32, one launch (start us, length us, event | category | flops | bytes accessed | tf_op | source)
XLA Modules:
  0.0 850.9 jit_solution(382479350491450475)
XLA Ops:
  8.3 7.4 collective-permute-start
  21.1 6.0 collective-permute-start.3
  27.0 5.2 collective-permute-start.4
  34.5 6.4 collective-permute-start.5
  44.6 11.4 %collective-permute-start.7 = (bf16[16,512]{1,0:T(8,128)(2,1)S(1)}, bf16[16,512]{1,0:T(8,128)(2,1)S(1)}, u32[]{:S(2)}, u32[]{:S(2)}) collective-permute-start(bf16[16,512]{1,0:T(8,128)(2,1)S(1)} %get-tuple-element.3222), channel_id=1, source_target_pairs={{0,8},{1,9},{2,10},{3,11},{4,12},{5,13},{6,14},{7,15},{8,0},{9,1},... | collective-permute-start | bytes 49160 | tf_op jit(solution)/shard_map/ppermute | solution.py:148
  65.7 6.4 collective-permute-start.10
  77.2 6.1 collective-permute-start.12
  83.4 5.6 collective-permute-start.13
  92.4 5.2 collective-permute-done.14
  103.6 63.1 %while.169 = (s32[]{:T(128)}, f32[2,128,128]{2,1,0:T(8,128)S(1)}, f32[2,128,128]{2,1,0:T(8,128)S(1)}, f32[4,2,64,128]{3,2,1,0:T(8,128)S(1)}, f32[4,2,64,1]{2,1,3...) while((s32[]{:T(128)}, f32[2,128,128]{2,1,0:T(8,128)S(1)}, ...), condition=%wide.region_4.6_spmd.clone.clone, body=%wide.region_2.5_spmd.clone.clone.sunk | while | flops 176640128 | bytes 2981140 | solution.py:86
  106.5 9.8 %custom-call.35 = f32[2,1,64,64]{2,3,1,0:T(8,128)S(1)} custom-call(f32[2,1,64,64]{3,2,1,0:T(8,128)S(1)} %fusion.420), custom_call_target="InvertDiagBlocksLowerTriangular" | custom-call | tf_op jit(solution)/shard_map/jvp(vmap())/while/body/eval_jaxpr/jit(_solve_triangular)/triangular_solve/custom-call.1 | solution.py:57
  122.3 9.8 %custom-call.35 = f32[2,1,64,64]{2,3,1,0:T(8,128)S(1)} custom-call(f32[2,1,64,64]{3,2,1,0:T(8,128)S(1)} %fusion.420), custom_call_target="InvertDiagBlocksLowerTriangular" | custom-call | tf_op jit(solution)/shard_map/jvp(vmap())/while/body/eval_jaxpr/jit(_solve_triangular)/triangular_solve/custom-call.1 | solution.py:57
  138.1 9.8 %custom-call.35 = f32[2,1,64,64]{2,3,1,0:T(8,128)S(1)} custom-call(f32[2,1,64,64]{3,2,1,0:T(8,128)S(1)} %fusion.420), custom_call_target="InvertDiagBlocksLowerTriangular" | custom-call | tf_op jit(solution)/shard_map/jvp(vmap())/while/body/eval_jaxpr/jit(_solve_triangular)/triangular_solve/custom-call.1 | solution.py:57
  153.9 9.8 %custom-call.35 = f32[2,1,64,64]{2,3,1,0:T(8,128)S(1)} custom-call(f32[2,1,64,64]{3,2,1,0:T(8,128)S(1)} %fusion.420), custom_call_target="InvertDiagBlocksLowerTriangular" | custom-call | tf_op jit(solution)/shard_map/jvp(vmap())/while/body/eval_jaxpr/jit(_solve_triangular)/triangular_solve/custom-call.1 | solution.py:57
  172.0 5.9 while.166
  179.9 49.5 %all-gather.9.cloned.1.call-done = f32[64,128,128]{2,1,0:T(8,128)} async-done(((f32[2,128,128]{2,1,0:T(8,128)}), f32[64,128,128]{2,1,0:T(8,128)}) %all-gather.9.cloned.1.call-update) | async-done | bytes 4194320 | tf_op jit(solution)/shard_map/all_gather | solution.py:24
  229.4 64.6 %all-gather.11.cloned.1.call-done = f32[64,128,128]{2,1,0:T(8,128)} async-done(((f32[2,128,128]{2,1,0:T(8,128)}), f32[64,128,128]{2,1,0:T(8,128)}) %all-gather.11.cloned.1.call-update) | async-done | bytes 4194320 | tf_op jit(solution)/shard_map/all_gather | solution.py:24
  294.0 80.1 %while.167 = (s32[]{:T(128)}, f32[2,128,128]{2,1,0:T(8,128)S(1)}, f32[2,128,128]{2,1,0:T(8,128)S(1)}, s32[]{:T(128)}, f32[32,2,128,128]{3,2,1,0:T(8,128)}, /*ind...) while((s32[]{:T(128)}, f32[2,128,128]{2,1,0:T(8,128)S(1)}, ...), condition=%wide.region_8.10_spmd.clone, body=%wide.region_7.9_spmd.clone.sunk | while | flops 100827144 | bytes 1706674 | solution.py:37
  374.2 47.8 %all-gather.15.cloned.1.call-done = f32[64,128,128]{2,1,0:T(8,128)} async-done(((f32[2,128,128]{2,1,0:T(8,128)}), f32[64,128,128]{2,1,0:T(8,128)}) %all-gather.15.cloned.1.call-update) | async-done | bytes 4194320 | tf_op jit(solution)/shard_map/all_gather | solution.py:24
  422.0 79.7 %while.168 = (s32[]{:T(128)}, f32[2,128,128]{2,1,0:T(8,128)S(1)}, f32[2,128,128]{2,1,0:T(8,128)S(1)}, s32[]{:T(128)}, f32[32,2,128,128]{3,2,1,0:T(8,128)}, /*ind...) while((s32[]{:T(128)}, f32[2,128,128]{2,1,0:T(8,128)S(1)}, f32[2,128,128]{2,1,0:T(8,128)S(1)}, ...), condition=%wide.region_10.12_spmd.clone, body=%wide.region_9.11_spmd.clone.sunk | while | flops 100827136 | bytes 1706612 | solution.py:37
  514.1 107.1 %while.164 = (s32[]{:T(128)}, f32[2,128,128]{2,1,0:T(8,128)S(1)}, f32[4,2,64,64]{3,2,1,0:T(8,128)}, f32[4,2,128,64]{2,3,1,0:T(8,128)}, f32[4,2,64,64]{3,2,1,0:T(...) while((s32[]{:T(128)}, f32[2,128,128]{2,1,0:T(8,128)S(1)}, ...), condition=%wide.region_13.15_spmd.clone.clone, body=%wide.region_11.14_spmd.clone.clone.sunk | while | flops 126194176 | bytes 3312057 | solution.py:86
  519.2 11.2 %custom-call.33 = f32[2,1,64,64]{2,3,1,0:T(8,128)} custom-call(f32[2,1,64,64]{3,2,1,0:T(8,128)} %select_bitcast_fusion.4), custom_call_target="InvertDiagBlocksLowerTriangular" | custom-call | tf_op jit(solution)/shard_map/jvp(vmap())/while/body/eval_jaxpr/jit(_solve_triangular)/triangular_solve/custom-call.1 | solution.py:57
  546.0 11.2 %custom-call.33 = f32[2,1,64,64]{2,3,1,0:T(8,128)} custom-call(f32[2,1,64,64]{3,2,1,0:T(8,128)} %select_bitcast_fusion.4), custom_call_target="InvertDiagBlocksLowerTriangular" | custom-call | tf_op jit(solution)/shard_map/jvp(vmap())/while/body/eval_jaxpr/jit(_solve_triangular)/triangular_solve/custom-call.1 | solution.py:57
  572.7 11.2 %custom-call.33 = f32[2,1,64,64]{2,3,1,0:T(8,128)} custom-call(f32[2,1,64,64]{3,2,1,0:T(8,128)} %select_bitcast_fusion.4), custom_call_target="InvertDiagBlocksLowerTriangular" | custom-call | tf_op jit(solution)/shard_map/jvp(vmap())/while/body/eval_jaxpr/jit(_solve_triangular)/triangular_solve/custom-call.1 | solution.py:57
  599.5 11.2 %custom-call.33 = f32[2,1,64,64]{2,3,1,0:T(8,128)} custom-call(f32[2,1,64,64]{3,2,1,0:T(8,128)} %select_bitcast_fusion.4), custom_call_target="InvertDiagBlocksLowerTriangular" | custom-call | tf_op jit(solution)/shard_map/jvp(vmap())/while/body/eval_jaxpr/jit(_solve_triangular)/triangular_solve/custom-call.1 | solution.py:57
  625.3 127.3 %while.165 = (s32[]{:T(128)}, f32[2,128,128]{2,1,0:T(8,128)S(1)}, f32[4,2,64,128]{3,2,1,0:T(8,128)}, f32[4,2,64,128]{3,2,1,0:T(8,128)}, f32[4,2,64,128]{3,2,0,1:...) while((s32[]{:T(128)}, f32[2,128,128]{2,1,0:T(8,128)S(1)}, ...), condition=%wide.region_25.27_spmd.clone.clone, body=%wide.region_14.26_spmd.clone.clone.sunk | while | flops 283857920 | bytes 5617773 | solution.py:86
  628.9 9.8 %custom-call.34 = f32[2,1,64,64]{2,3,1,0:T(8,128)S(1)} custom-call(f32[2,1,64,64]{3,2,1,0:T(8,128)S(1)} %select_bitcast_fusion.5), custom_call_target="InvertDiagBlocksLowerTriangular" | custom-call | tf_op jit(solution)/shard_map/transpose(jvp(vmap()))/while/body/eval_jaxpr/jit(_solve_triangular)/triangular_solve | solution.py:57
  660.7 9.8 %custom-call.34 = f32[2,1,64,64]{2,3,1,0:T(8,128)S(1)} custom-call(f32[2,1,64,64]{3,2,1,0:T(8,128)S(1)} %select_bitcast_fusion.5), custom_call_target="InvertDiagBlocksLowerTriangular" | custom-call | tf_op jit(solution)/shard_map/transpose(jvp(vmap()))/while/body/eval_jaxpr/jit(_solve_triangular)/triangular_solve | solution.py:57
  692.5 9.8 %custom-call.34 = f32[2,1,64,64]{2,3,1,0:T(8,128)S(1)} custom-call(f32[2,1,64,64]{3,2,1,0:T(8,128)S(1)} %select_bitcast_fusion.5), custom_call_target="InvertDiagBlocksLowerTriangular" | custom-call | tf_op jit(solution)/shard_map/transpose(jvp(vmap()))/while/body/eval_jaxpr/jit(_solve_triangular)/triangular_solve | solution.py:57
  724.3 9.8 %custom-call.34 = f32[2,1,64,64]{2,3,1,0:T(8,128)S(1)} custom-call(f32[2,1,64,64]{3,2,1,0:T(8,128)S(1)} %select_bitcast_fusion.5), custom_call_target="InvertDiagBlocksLowerTriangular" | custom-call | tf_op jit(solution)/shard_map/transpose(jvp(vmap()))/while/body/eval_jaxpr/jit(_solve_triangular)/triangular_solve | solution.py:57
  763.1 12.7 %all-to-all-start = ((bf16[16,16,512]{2,1,0:T(8,128)(2,1)}), bf16[16,16,512]{2,1,0:T(8,128)(2,1)S(1)}, u32[]{:S(2)}, u32[]{:S(2)}) async-start(bf16[16,16,512]{2,1,0:T(8,128)(2,1)} %bitcast.31), calls=%async_computation | async-start | bytes 524288 | tf_op jit(solution)/shard_map/all_to_all | solution.py:181
  776.6 66.4 %psum.7 = f32[4,512]{1,0:T(4,128)} all-reduce(f32[4,512]{1,0:T(4,128)S(1)} %pad_add_fusion.5), channel_id=1, replica_groups=mesh['ctx'=32,'head'=16] {'ctx'}, use_global_device_ids=true, to_apply=%region_34.36 | all-reduce | flops 2048 | bytes 16384 | tf_op jit(solution)/shard_map/psum | solution.py:184
  (782 shorter events, 406.6 us)
Async XLA Ops:
  7.2 494.6 %copy-start = (f32[2,128,128]{2,1,0:T(8,128)S(1)}, f32[2,128,128]{2,1,0:T(8,128)}, u32[]{:S(2)}) copy-start(f32[2,128,128]{2,1,0:T(8,128)} %param.25) | copy-start | bytes 393220
  7.2 222.2 %all-gather.9.cloned.1.call-start = ((), (), s32[]{:S(2)}) async-start(), calls=%async_computation.1 | async-start | bytes 4325376 | tf_op jit(solution)/shard_map/all_gather | solution.py:24
  8.3 26.1 %collective-permute-start = (bf16[16,512]{1,0:T(8,128)(2,1)S(1)}, bf16[16,512]{1,0:T(8,128)(2,1)S(1)}, u32[]{:S(2)}, u32[]{:S(2)}) collective-permute-start(bf16[16,512]{1,0:T(8,128)(2,1)S(1)} %get-tuple-element.3229), channel_id=1, source_target_pairs={{0,1},{1,0},{2,3},{3,2},{4,5},{5,4},{6,7},{7,6},{8,9},{9,8},{10,11... | collective-permute-start | bytes 49160 | tf_op jit(solution)/shard_map/ppermute | solution.py:148
  15.7 25.2 %collective-permute-start.1 = (bf16[16,512]{1,0:T(8,128)(2,1)S(1)}, bf16[16,512]{1,0:T(8,128)(2,1)S(1)}, u32[]{:S(2)}, u32[]{:S(2)}) collective-permute-start(bf16[16,512]{1,0:T(8,128)(2,1)S(1)} %get-tuple-element.3228), channel_id=1, source_target_pairs={{0,2},{1,3},{2,0},{3,1},{4,6},{5,7},{6,4},{7,5},{8,10},{9,11},{10,... | collective-permute-start | bytes 49160 | tf_op jit(solution)/shard_map/ppermute | solution.py:148
  17.7 27.0 %collective-permute-start.2 = (bf16[16,512]{1,0:T(8,128)(2,1)S(1)}, bf16[16,512]{1,0:T(8,128)(2,1)S(1)}, u32[]{:S(2)}, u32[]{:S(2)}) collective-permute-start(bf16[16,512]{1,0:T(8,128)(2,1)S(1)} %get-tuple-element.3227), channel_id=1, source_target_pairs={{0,3},{1,2},{2,1},{3,0},{4,7},{5,6},{6,5},{7,4},{8,11},{9,10},{10,... | collective-permute-start | bytes 49160 | tf_op jit(solution)/shard_map/ppermute | solution.py:148
  21.1 35.0 %collective-permute-start.3 = (bf16[16,512]{1,0:T(8,128)(2,1)S(1)}, bf16[16,512]{1,0:T(8,128)(2,1)S(1)}, u32[]{:S(2)}, u32[]{:S(2)}) collective-permute-start(bf16[16,512]{1,0:T(8,128)(2,1)S(1)} %get-tuple-element.3226), channel_id=1, source_target_pairs={{0,4},{1,5},{2,6},{3,7},{4,0},{5,1},{6,2},{7,3},{8,12},{9,13},{10,... | collective-permute-start | bytes 49160 | tf_op jit(solution)/shard_map/ppermute | solution.py:148
  27.0 33.7 %collective-permute-start.4 = (bf16[16,512]{1,0:T(8,128)(2,1)S(1)}, bf16[16,512]{1,0:T(8,128)(2,1)S(1)}, u32[]{:S(2)}, u32[]{:S(2)}) collective-permute-start(bf16[16,512]{1,0:T(8,128)(2,1)S(1)} %get-tuple-element.3225), channel_id=1, source_target_pairs={{0,5},{1,4},{2,7},{3,6},{4,1},{5,0},{6,3},{7,2},{8,13},{9,12},{10,... | collective-permute-start | bytes 49160 | tf_op jit(solution)/shard_map/ppermute | solution.py:148
  33.1 70.3 %copy-start.7 = (f32[1,512]{1,0:T(1,128)}, f32[1,512]{1,0:T(1,128)S(1)}, u32[]{:S(2)}) copy-start(f32[1,512]{1,0:T(1,128)S(1)} %get-tuple-element.3232) | copy-start | bytes 6148
  33.2 70.3 %copy-start.9 = (f32[1,512]{1,0:T(1,128)}, f32[1,512]{1,0:T(1,128)S(1)}, u32[]{:S(2)}) copy-start(f32[1,512]{1,0:T(1,128)S(1)} %get-tuple-element.3233) | copy-start | bytes 6148
  33.2 70.3 %copy-start.11 = (f32[1,512]{1,0:T(1,128)}, f32[1,512]{1,0:T(1,128)S(1)}, u32[]{:S(2)}) copy-start(f32[1,512]{1,0:T(1,128)S(1)} %get-tuple-element.3234) | copy-start | bytes 6148
  33.2 70.3 %copy-start.13 = (f32[1,512]{1,0:T(1,128)}, f32[1,512]{1,0:T(1,128)S(1)}, u32[]{:S(2)}) copy-start(f32[1,512]{1,0:T(1,128)S(1)} %get-tuple-element.3235) | copy-start | bytes 6148
  34.5 31.2 %collective-permute-start.5 = (bf16[16,512]{1,0:T(8,128)(2,1)S(1)}, bf16[16,512]{1,0:T(8,128)(2,1)S(1)}, u32[]{:S(2)}, u32[]{:S(2)}) collective-permute-start(bf16[16,512]{1,0:T(8,128)(2,1)S(1)} %get-tuple-element.3224), channel_id=1, source_target_pairs={{0,6},{1,7},{2,4},{3,5},{4,2},{5,3},{6,0},{7,1},{8,14},{9,15},{10,... | collective-permute-start | bytes 49160 | tf_op jit(solution)/shard_map/ppermute | solution.py:148
  40.9 31.2 %collective-permute-start.6 = (bf16[16,512]{1,0:T(8,128)(2,1)S(1)}, bf16[16,512]{1,0:T(8,128)(2,1)S(1)}, u32[]{:S(2)}, u32[]{:S(2)}) collective-permute-start(bf16[16,512]{1,0:T(8,128)(2,1)S(1)} %get-tuple-element.3223), channel_id=1, source_target_pairs={{0,7},{1,6},{2,5},{3,4},{4,3},{5,2},{6,1},{7,0},{8,15},{9,14},{10,... | collective-permute-start | bytes 49160 | tf_op jit(solution)/shard_map/ppermute | solution.py:148
  44.6 32.6 %collective-permute-start.7 = (bf16[16,512]{1,0:T(8,128)(2,1)S(1)}, bf16[16,512]{1,0:T(8,128)(2,1)S(1)}, u32[]{:S(2)}, u32[]{:S(2)}) collective-permute-start(bf16[16,512]{1,0:T(8,128)(2,1)S(1)} %get-tuple-element.3222), channel_id=1, source_target_pairs={{0,8},{1,9},{2,10},{3,11},{4,12},{5,13},{6,14},{7,15},{8,0},{9,1},... | collective-permute-start | bytes 49160 | tf_op jit(solution)/shard_map/ppermute | solution.py:148
  56.0 27.3 %collective-permute-start.8 = (bf16[16,512]{1,0:T(8,128)(2,1)S(1)}, bf16[16,512]{1,0:T(8,128)(2,1)S(1)}, u32[]{:S(2)}, u32[]{:S(2)}) collective-permute-start(bf16[16,512]{1,0:T(8,128)(2,1)S(1)} %get-tuple-element.3221), channel_id=1, source_target_pairs={{0,9},{1,8},{2,11},{3,10},{4,13},{5,12},{6,15},{7,14},{8,1},{9,0},... | collective-permute-start | bytes 49160 | tf_op jit(solution)/shard_map/ppermute | solution.py:148
  60.7 28.3 %collective-permute-start.9 = (bf16[16,512]{1,0:T(8,128)(2,1)S(1)}, bf16[16,512]{1,0:T(8,128)(2,1)S(1)}, u32[]{:S(2)}, u32[]{:S(2)}) collective-permute-start(bf16[16,512]{1,0:T(8,128)(2,1)S(1)} %get-tuple-element.3220), channel_id=1, source_target_pairs={{0,10},{1,11},{2,8},{3,9},{4,14},{5,15},{6,12},{7,13},{8,2},{9,3},... | collective-permute-start | bytes 49160 | tf_op jit(solution)/shard_map/ppermute | solution.py:148
  65.7 26.6 %collective-permute-start.10 = (bf16[16,512]{1,0:T(8,128)(2,1)S(1)}, bf16[16,512]{1,0:T(8,128)(2,1)S(1)}, u32[]{:S(2)}, u32[]{:S(2)}) collective-permute-start(bf16[16,512]{1,0:T(8,128)(2,1)S(1)} %get-tuple-element.3219), channel_id=1, source_target_pairs={{0,11},{1,10},{2,9},{3,8},{4,15},{5,14},{6,13},{7,12},{8,3},{9,2},... | collective-permute-start | bytes 49160 | tf_op jit(solution)/shard_map/ppermute | solution.py:148
  72.2 20.1 %collective-permute-start.11 = (bf16[16,512]{1,0:T(8,128)(2,1)S(1)}, bf16[16,512]{1,0:T(8,128)(2,1)S(1)}, u32[]{:S(2)}, u32[]{:S(2)}) collective-permute-start(bf16[16,512]{1,0:T(8,128)(2,1)S(1)} %get-tuple-element.3218), channel_id=1, source_target_pairs={{0,12},{1,13},{2,14},{3,15},{4,8},{5,9},{6,10},{7,11},{8,4},{9,5},... | collective-permute-start | bytes 49160 | tf_op jit(solution)/shard_map/ppermute | solution.py:148
  77.2 15.1 %collective-permute-start.12 = (bf16[16,512]{1,0:T(8,128)(2,1)S(1)}, bf16[16,512]{1,0:T(8,128)(2,1)S(1)}, u32[]{:S(2)}, u32[]{:S(2)}) collective-permute-start(bf16[16,512]{1,0:T(8,128)(2,1)S(1)} %get-tuple-element.3217), channel_id=1, source_target_pairs={{0,13},{1,12},{2,15},{3,14},{4,9},{5,8},{6,11},{7,10},{8,5},{9,4},... | collective-permute-start | bytes 49160 | tf_op jit(solution)/shard_map/ppermute | solution.py:148
  83.4 9.0 %collective-permute-start.13 = (bf16[16,512]{1,0:T(8,128)(2,1)S(1)}, bf16[16,512]{1,0:T(8,128)(2,1)S(1)}, u32[]{:S(2)}, u32[]{:S(2)}) collective-permute-start(bf16[16,512]{1,0:T(8,128)(2,1)S(1)} %get-tuple-element.3231), channel_id=1, source_target_pairs={{0,14},{1,15},{2,12},{3,13},{4,10},{5,11},{6,8},{7,9},{8,6},{9,7},... | collective-permute-start | bytes 49160 | tf_op jit(solution)/shard_map/ppermute | solution.py:148
  89.0 8.6 %collective-permute-start.14 = (bf16[16,512]{1,0:T(8,128)(2,1)S(1)}, bf16[16,512]{1,0:T(8,128)(2,1)S(1)}, u32[]{:S(2)}, u32[]{:S(2)}) collective-permute-start(bf16[16,512]{1,0:T(8,128)(2,1)S(1)} %get-tuple-element.3216), channel_id=1, source_target_pairs={{0,15},{1,14},{2,13},{3,12},{4,11},{5,10},{6,9},{7,8},{8,7},{9,6},... | collective-permute-start | bytes 49160 | tf_op jit(solution)/shard_map/ppermute | solution.py:148
  97.6 3.4 collective-permute-start.15
  167.5 126.5 %all-gather.11.cloned.1.call-start = ((), (), s32[]{:S(2)}) async-start(), calls=%async_computation.2 | async-start | bytes 4325376 | tf_op jit(solution)/shard_map/all_gather | solution.py:24
  178.5 195.6 %all-gather.13.cloned.1.call-start = ((), (), s32[]{:S(2)}) async-start(), calls=%async_computation.3 | async-start | bytes 4325376 | tf_op jit(solution)/shard_map/all_gather | solution.py:24
  179.3 242.7 %all-gather.15.cloned.1.call-start = ((), (), s32[]{:S(2)}) async-start(), calls=%async_computation.4 | async-start | bytes 4325376 | tf_op jit(solution)/shard_map/all_gather | solution.py:24
  374.1 47.9 %copy-start.4 = (f32[2,128,128]{2,1,0:T(8,128)}, f32[2,128,128]{2,1,0:T(8,128)S(1)}, u32[]{:S(2)}) copy-start(f32[2,128,128]{2,1,0:T(8,128)S(1)} %get-tuple-element.2004) | copy-start | bytes 393220
  625.3 30.1 %copy-start.5 = (f32[4,2,64]{2,1,0:T(2,128)S(1)}, f32[4,2,64]{2,1,0:T(2,128)}, u32[]{:S(2)}) copy-start(f32[4,2,64]{2,1,0:T(2,128)} %get-tuple-element.4312) | copy-start | bytes 6148 | tf_op jit(solution)/shard_map/transpose(jvp(vmap()))/while
  657.1 30.1 %copy-start.5 = (f32[4,2,64]{2,1,0:T(2,128)S(1)}, f32[4,2,64]{2,1,0:T(2,128)}, u32[]{:S(2)}) copy-start(f32[4,2,64]{2,1,0:T(2,128)} %get-tuple-element.4312) | copy-start | bytes 6148 | tf_op jit(solution)/shard_map/transpose(jvp(vmap()))/while
  720.7 30.0 %copy-start.5 = (f32[4,2,64]{2,1,0:T(2,128)S(1)}, f32[4,2,64]{2,1,0:T(2,128)}, u32[]{:S(2)}) copy-start(f32[4,2,64]{2,1,0:T(2,128)} %get-tuple-element.4312) | copy-start | bytes 6148 | tf_op jit(solution)/shard_map/transpose(jvp(vmap()))/while
  759.3 83.7 %copy-start.19 = (f32[2,256]{1,0:T(2,128)S(1)}, f32[2,256]{1,0:T(2,128)}, u32[]{:S(2)}) copy-start(f32[2,256]{1,0:T(2,128)} %param.23) | copy-start | bytes 6148
  759.3 3.1 collective-permute-start.16
  763.1 80.5 %all-to-all-start = ((bf16[16,16,512]{2,1,0:T(8,128)(2,1)}), bf16[16,16,512]{2,1,0:T(8,128)(2,1)S(1)}, u32[]{:S(2)}, u32[]{:S(2)}) async-start(bf16[16,16,512]{2,1,0:T(8,128)(2,1)} %bitcast.31), calls=%async_computation | async-start | bytes 524288 | tf_op jit(solution)/shard_map/all_to_all | solution.py:181
  (16 other events, 205.3 us)
Sparse Core Ops, SparseCore 0:
  167.6 61.7 all-gather.8
  233.1 60.8 all-gather.10
  297.1 60.9 all-gather.12
  361.1 60.8 all-gather.14
